TPU v7x, 32 devices: a whole 2x2x4 slice. The times are simulated.
32 devices in a mesh: grp: 2 (over x), feed: 16 (over z, y, core).
Axes of the slice: x: 2, y: 2, z: 4, core: 2. Of those that a mesh axis runs over, the one named last changes fastest.
Arguments:
- samples: bfloat16 [32, 256, 65536], P(('grp', 'feed')), parts along dimension 0, may hold values from -6 to 6
- pfb_taps: float32 [4, 8192], replicated, may hold values from -0.03125 to 0.03125
Outputs:
- visibility: float32 [16384, 4096], P(('grp', 'feed')), parts along dimension 0
There are 2 independent parts, one for each index of `grp`. A program takes and returns all parts, laid end to end along the dimension named above; an argument that names none is the same for every part. Nothing has to cross between parts.
All inputs are finite; a program needn't handle non-finite values.
Results may differ from a plain program's by a relative error of at most 0.004.
Values may be sent and summed in bfloat16 or wider, within the bound.
A program may use at most 192 MiB of HBM per device.

v0:
```python
import math

import jax
import jax.numpy as jnp
from jax import lax
from jax.sharding import PartitionSpec as P

FIRST_CH = 1536
TIME_BLOCKS = 2
ROWS_DEV = 512


def passed_along(value, axis, steps):
    count = lax.axis_size(axis)
    first, last = (max(0, -steps), min(count, count - steps))
    return lax.ppermute(value, axis, [(source, source + steps) for source in range(first, last)])


def dft_matrix(fft_len, first_channel, channel_count):
    sample_ids = jnp.arange(fft_len, dtype=jnp.int32)
    channel_ids = first_channel + jnp.arange(channel_count, dtype=jnp.int32)
    phase = sample_ids[:, None] * channel_ids[None, :] % fft_len
    angle = phase.astype(jnp.float32) * (2.0 * math.pi / fft_len)
    return jnp.concatenate([jnp.cos(angle), -jnp.sin(angle)], axis=1)


def filter_sum(extended, pfb_taps, count):
    tap_count = pfb_taps.shape[0]
    total = jnp.zeros((extended.shape[0], count, extended.shape[2]), jnp.float32)
    for tap_index in range(tap_count):
        total = (
            total
            + extended[:, tap_index : tap_index + count].astype(jnp.float32) * pfb_taps[tap_index]
        )
    return total


def apply_table(filtered, dft_table):
    feed_count, count, fft_len = filtered.shape
    product = jnp.dot(
        filtered.reshape(feed_count * count, fft_len),
        dft_table,
        precision=lax.Precision.HIGHEST,
        preferred_element_type=jnp.float32,
    )
    return product.reshape(feed_count, count, -1)


def body(samples, pfb_taps):
    feed_count = samples.shape[1]
    tap_count, fft_len = pfb_taps.shape
    frame_count = samples.shape[2] // fft_len
    devices = lax.axis_size("feed")
    my_index = lax.axis_index("feed")
    group_span = devices // TIME_BLOCKS
    total_feeds = feed_count * group_span
    channels = devices * ROWS_DEV // total_feeds
    owners = total_feeds // ROWS_DEV
    spectra_count = TIME_BLOCKS * frame_count
    later_block = my_index >= group_span
    frames = samples.reshape(feed_count, frame_count, fft_len)
    dft_table = dft_matrix(fft_len, FIRST_CH, channels)
    edge = tap_count - 1
    tail_frames = frames[:, frame_count - edge :]
    shifted = passed_along(tail_frames, "feed", group_span)
    before = jnp.where(later_block, shifted, jnp.zeros_like(shifted))
    extended = jnp.concatenate([before, frames], axis=1)
    spectra = apply_table(filter_sum(extended, pfb_taps, frame_count), dft_table)
    spectra = spectra.astype(jnp.bfloat16)
    per_channel = jnp.transpose(spectra.reshape(feed_count, frame_count, 2, channels), (3, 0, 2, 1))
    outgoing_all = jnp.repeat(
        per_channel.reshape(channels, feed_count, 2 * frame_count), owners, axis=0
    )
    gathered = lax.all_to_all(outgoing_all, "feed", split_axis=0, concat_axis=0, tiled=True)
    arranged = gathered.reshape(TIME_BLOCKS, group_span, feed_count, 2, frame_count)
    all_feeds = jnp.transpose(arranged, (1, 2, 3, 0, 4)).reshape(total_feeds, 2 * spectra_count)
    real_part = all_feeds[:, :spectra_count]
    imag_part = all_feeds[:, spectra_count:]
    right_matrix = jnp.concatenate(
        [all_feeds, jnp.concatenate([-imag_part, real_part], axis=1)], axis=0
    ).T
    row_start = my_index % owners * ROWS_DEV
    left_rows = lax.dynamic_slice_in_dim(all_feeds, row_start, ROWS_DEV, 0)
    visibility = jnp.dot(left_rows, right_matrix, preferred_element_type=jnp.float32) * (
        1.0 / spectra_count
    )
    return visibility


def solution(mesh):
    placed = (P(("grp", "feed"), None, None), P())
    return jax.shard_map(
        body, mesh=mesh, in_specs=placed, out_specs=P(("grp", "feed"), None), check_vma=False
    )
```

profile of v0, /device:TPU:0, one launch (start us, length us, event | category | flops | bytes accessed | tf_op | source)
XLA Modules:
  0.0 726.7 jit_solution(738564118373659306)
XLA Ops:
  0.0 29.2 %copy.11 = bf16[32,8,8,8192]{3,2,1,0:T(8,128)(2,1)} copy(bf16[32,8,8,8192]{3,1,2,0:T(8,128)(2,1)} %bitcast.30) | data formatting | bytes 67108864
  29.2 0.0 copy-start
  29.2 29.4 %copy.6 = bf16[256,8,8192]{2,0,1:T(8,128)(2,1)} copy(bf16[256,8,8192]{2,1,0:T(8,128)(2,1)} %bitcast.29) | data formatting | bytes 67108864 | tf_op jit(solution)/shard_map/reshape | solution.py:61
  58.6 10.5 %slice.40 = bf16[256,3,8192]{2,0,1:T(8,128)(2,1)} slice(bf16[256,8,8192]{2,0,1:T(8,128)(2,1)} %copy.6), slice={[0:256], [5:8], [0:8192]} | slice | bytes 25165824 | tf_op jit(solution)/shard_map/slice | solution.py:64
  69.1 10.4 %collective-permute-start = (bf16[256,3,8192]{2,0,1:T(8,128)(2,1)}, bf16[256,3,8192]{2,0,1:T(8,128)(2,1)}, u32[]{:S(2)}, u32[]{:S(2)}) collective-permute-start(bf16[256,3,8192]{2,0,1:T(8,128)(2,1)} %slice.40), channel_id=1, source_target_pairs={{0,8},{1,9},{2,10},{3,11},{4,12},{5,13},{6,14},{7,15},{16,24},{17,... | collective-permute-start | bytes 37748744 | tf_op jit(solution)/shard_map/ppermute | solution.py:16
  79.5 0.0 copy-done
  79.5 0.1 fusion.40
  79.6 1.2 fusion.34
  80.8 264.1 %collective-permute-done = bf16[256,3,8192]{2,0,1:T(8,128)(2,1)} collective-permute-done((bf16[256,3,8192]{2,0,1:T(8,128)(2,1)}, bf16[256,3,8192]{2,0,1:T(8,128)(2,1)}, u32[]{:S(2)}, u32[]{:S(2)}) %collective-permute-start) | collective-permute-done | bytes 12582944 | tf_op jit(solution)/shard_map/ppermute | solution.py:16
  345.0 1.0 broadcast_select_fusion
  345.9 86.0 %fusion.21 = bf16[256,8,8]{0,2,1:T(8,128)(2,1)S(1)} fusion(bf16[256,8,8192]{2,0,1:T(8,128)(2,1)} %copy.6, bf16[256,3,8192]{2,0,1:T(8,128)(2,1)S(1)} %broadcast_select_fusion, f32[8192]{0:T(1024)S(1)} %bitcast.38, f32[8192]{0:T(1024)S(1)} %bitcast.39, f32[8192]{0:T(1024)S(1)} %bitcast.37, f32[8192]{0:T(1024)S(1)} %bitcast.36, ...), kind=kOutput, calls=%fused_computation.26 | convolution fusion | flops 1845575680 | bytes 46563328 | tf_op jit(solution)/shard_map/dot_general | solution.py:40
  431.9 0.7 broadcast_in_dim.9
  432.6 281.4 %all-to-all-start = ((bf16[16,256,16]{1,2,0:T(8,128)(2,1)}), bf16[16,256,16]{1,2,0:T(8,128)(2,1)S(1)}, u32[]{:S(2)}, u32[]{:S(2)}) async-start(bf16[16,256,16]{1,2,0:T(8,128)(2,1)} %bitcast.7), calls=%async_computation | async-start | bytes 262144 | tf_op jit(solution)/shard_map/all_to_all | solution.py:74
  714.0 7.9 %all-to-all-done = bf16[16,256,16]{1,2,0:T(8,128)(2,1)S(1)} async-done(((bf16[16,256,16]{1,2,0:T(8,128)(2,1)}), bf16[16,256,16]{1,2,0:T(8,128)(2,1)S(1)}, u32[]{:S(2)}, u32[]{:S(2)}) %all-to-all-start) | async-done | bytes 131104 | tf_op jit(solution)/shard_map/all_to_all | solution.py:74
  722.0 4.7 convolution_multiply_fusion
  (6 shorter events, 0.1 us)
Async XLA Ops:
  29.2 50.3 %copy-start = (f32[4,8192]{1,0:T(4,128)S(1)}, f32[4,8192]{1,0:T(4,128)}, u32[]{:S(2)}) copy-start(f32[4,8192]{1,0:T(4,128)} %param.3) | copy-start | bytes 393220
  69.1 275.9 %collective-permute-start = (bf16[256,3,8192]{2,0,1:T(8,128)(2,1)}, bf16[256,3,8192]{2,0,1:T(8,128)(2,1)}, u32[]{:S(2)}, u32[]{:S(2)}) collective-permute-start(bf16[256,3,8192]{2,0,1:T(8,128)(2,1)} %slice.40), channel_id=1, source_target_pairs={{0,8},{1,9},{2,10},{3,11},{4,12},{5,13},{6,14},{7,15},{16,24},{17,... | collective-permute-start | bytes 37748744 | tf_op jit(solution)/shard_map/ppermute | solution.py:16
  432.6 289.3 %all-to-all-start = ((bf16[16,256,16]{1,2,0:T(8,128)(2,1)}), bf16[16,256,16]{1,2,0:T(8,128)(2,1)S(1)}, u32[]{:S(2)}, u32[]{:S(2)}) async-start(bf16[16,256,16]{1,2,0:T(8,128)(2,1)} %bitcast.7), calls=%async_computation | async-start | bytes 262144 | tf_op jit(solution)/shard_map/all_to_all | solution.py:74
where the time goes:
time: 727 us
  starting transfers between devices  292 us (40%)
  waiting for transfers between devices  272 us (37%)
  matrix products  90.6 us (12%)
  local copies, waits for them, and re-layouts  69.9 us (10%)
    all_to_all x1, starting transfers between devices, body(): lax.all_to_all(outgoing_all, 'feed', split_axis=0, concat_axis=0, tiled=T...  281 us
    ppermute x1, waiting for transfers between devices, passed_along(): lax.ppermute(value, axis, [(source, source + steps) for source in range(f...  264 us
    dot_general x1, matrix products, apply_table(): jnp.dot(filtered.reshape(feed_count * count, fft_len), dft_table, precisi...  86 us
    reshape x1, local copies, waits for them, and re-layouts, body(): frames = samples.reshape(feed_count, frame_count, fft_len)  29.4 us
    unnamed x4, local copies, waits for them, and re-layouts  29.2 us
  transfers between devices with their start and end apart: 2, of which 2 were waited for; matrix products, arithmetic and copies ran while one was open for 0% of the time, Pallas kernels for 0%

commit v1 on v0

v1 whole, which is shorter than its diff:
```python
import functools
import math

import jax
import jax.numpy as jnp
import numpy as np
from jax import lax
from jax.experimental import pallas as pl
from jax.experimental.pallas import tpu as pltpu
from jax.sharding import PartitionSpec as P

FIRST_CH = 1536
TIME_BLOCKS = 2
ROWS_DEV = 512
PARTS = 3
CHUNKS = 4


def dft_rows(fft_len, channels):
    phase = (np.arange(fft_len)[None, :] * (FIRST_CH + np.arange(channels))[:, None]) % fft_len
    angle = phase * (2.0 * math.pi / fft_len)
    return np.concatenate([np.cos(angle), -np.sin(angle)], axis=0).astype(np.float32)


def channelize_kernel(
    devices, samples_ref, taps_ref, table_ref, out_ref,
    frames_buf, taps_buf, table_buf, w_buf, g_buf, spec_buf, msg_buf, spill_out, spill_in,
    load_sems, aux_sems, spill_sems, send_sems, recv_sems, own_sem,
):
    me = lax.axis_index("feed")
    span = devices // TIME_BLOCKS
    frame_count, feeds, fft_len = frames_buf.shape
    tap_count = taps_buf.shape[0]
    cols = table_buf.shape[0]
    channels = cols // 2
    owners = devices // channels
    edge = tap_count - 1
    chunk = fft_len // CHUNKS
    early = frame_count - edge

    aux = [
        pltpu.make_async_copy(taps_ref, taps_buf, aux_sems.at[0]),
        pltpu.make_async_copy(table_ref, table_buf, aux_sems.at[1]),
    ]
    for copy in aux:
        copy.start()

    def load(frame, part):
        start = pl.multiple_of(frame * fft_len + part * chunk, 128)
        return pltpu.make_async_copy(
            samples_ref.at[0, :, pl.ds(start, chunk)],
            frames_buf.at[frame, :, pl.ds(part * chunk, chunk)],
            load_sems.at[frame * CHUNKS + part],
        )

    def start_frame(step, carry):
        frame = lax.rem(step + early, frame_count)
        for part in range(CHUNKS):
            load(frame, part).start()
        return carry

    lax.fori_loop(0, frame_count, start_frame, 0)

    barrier = pltpu.get_barrier_semaphore()

    def greet(step, carry):
        peer = lax.rem(me + step, devices)
        pl.semaphore_signal(barrier, inc=1, device_id={"feed": peer}, device_id_type=pl.DeviceIdType.MESH)
        return carry

    lax.fori_loop(1, devices, greet, 0)

    for copy in aux:
        copy.wait()
    for tap in range(tap_count):
        rest = taps_buf[tap : tap + 1, :] * table_buf[...]
        for part in range(PARTS):
            piece = rest.astype(jnp.bfloat16)
            row = (part * tap_count + tap) * cols
            w_buf[row : row + cols, :] = piece
            rest = rest - piece.astype(jnp.float32)

    pl.semaphore_wait(barrier, devices - 1)

    def do_frame(frame, carry):
        total = None
        for part in range(CHUNKS):
            load(frame, part).wait()
            columns = slice(part * chunk, (part + 1) * chunk)
            product = lax.dot_general(
                w_buf[:, columns], frames_buf[frame, :, columns],
                (((1,), (1,)), ((), ())), preferred_element_type=jnp.float32,
            )
            total = product if total is None else total + product
        rows = tap_count * cols
        summed = total[:rows]
        for part in range(1, PARTS):
            summed = summed + total[part * rows : (part + 1) * rows]
        g_buf[frame] = summed
        return carry

    lax.fori_loop(early, frame_count, do_frame, 0)

    for later in range(edge):
        total = g_buf[early + later, 0:cols, :]
        for tap in range(1, edge - later):
            total = total + g_buf[early + later + tap, tap * cols : (tap + 1) * cols, :]
        spill_out[later] = total
    spill = pltpu.make_async_remote_copy(
        src_ref=spill_out, dst_ref=spill_in, send_sem=spill_sems.at[0], recv_sem=spill_sems.at[1],
        device_id={"feed": lax.rem(me + span, devices)}, device_id_type=pl.DeviceIdType.MESH,
    )

    @pl.when(me < span)
    def _():
        spill.start()
        spill_in[...] = jnp.zeros_like(spill_in)

    lax.fori_loop(0, early, do_frame, 0)

    @pl.when(me < span)
    def _():
        spill.wait_send()

    @pl.when(me >= span)
    def _():
        spill.wait_recv()

    for time in range(frame_count):
        total = spill_in[time] if time < edge else None
        for tap in range(tap_count):
            frame = time - edge + tap
            if frame >= 0:
                term = g_buf[frame, tap * cols : (tap + 1) * cols, :]
                total = term if total is None else total + term
        spec_buf[:, time, :] = total
    for channel in range(channels):
        msg_buf[channel] = jnp.concatenate(
            [spec_buf[channel], spec_buf[channels + channel]], axis=0
        ).astype(jnp.bfloat16)

    own = pltpu.make_async_copy(msg_buf.at[me // owners], out_ref.at[me], own_sem)

    def message(peer, slot, source):
        return pltpu.make_async_remote_copy(
            src_ref=msg_buf.at[peer // owners], dst_ref=out_ref.at[source],
            send_sem=send_sems.at[slot], recv_sem=recv_sems.at[slot],
            device_id={"feed": peer}, device_id_type=pl.DeviceIdType.MESH,
        )

    def send(step, carry):
        message(lax.rem(me + step, devices), step, me).start()
        return carry

    def finish(step, carry):
        copy = message(lax.rem(me + step, devices), step, lax.rem(me + devices - step, devices))
        copy.wait_send()
        copy.wait_recv()
        return carry

    lax.fori_loop(1, devices, send, 0)
    own.start()
    lax.fori_loop(1, devices, finish, 0)
    own.wait()


def correlate_kernel(devices, gathered_ref, out_ref, right_buf):
    _, depth, feeds = gathered_ref.shape
    half = depth // 2
    span = devices // TIME_BLOCKS
    total_feeds = span * feeds
    owners = total_feeds // ROWS_DEV
    rows = out_ref.shape[0]
    me = lax.axis_index("feed")
    spectra_count = TIME_BLOCKS * half

    @pl.when(pl.program_id(0) == 0)
    def _():
        for block in range(TIME_BLOCKS):
            for group in range(span):
                piece = gathered_ref[block * span + group]
                wide = piece.astype(jnp.float32)
                turned = jnp.concatenate([-wide[half:], wide[:half]], axis=0).astype(jnp.bfloat16)
                lines = slice(block * depth, (block + 1) * depth)
                right_buf[lines, group * feeds : (group + 1) * feeds] = piece
                right_buf[lines, total_feeds + group * feeds : total_feeds + (group + 1) * feeds] = turned

    start = pl.multiple_of(lax.rem(me, owners) * ROWS_DEV + pl.program_id(0) * rows, 128)
    left = right_buf[:, pl.ds(start, rows)]
    out_ref[...] = lax.dot_general(
        left, right_buf[...], (((0,), (0,)), ((), ())), preferred_element_type=jnp.float32
    ) * (1.0 / spectra_count)


def body(samples, pfb_taps):
    feeds = samples.shape[1]
    tap_count, fft_len = pfb_taps.shape
    frame_count = samples.shape[2] // fft_len
    devices = lax.axis_size("feed")
    total_feeds = feeds * (devices // TIME_BLOCKS)
    channels = devices * ROWS_DEV // total_feeds
    cols = 2 * channels
    edge = tap_count - 1
    table = jnp.asarray(dft_rows(fft_len, channels))
    anywhere = pl.BlockSpec(memory_space=pl.ANY)
    gathered = pl.pallas_call(
        functools.partial(channelize_kernel, devices),
        out_shape=jax.ShapeDtypeStruct((devices, 2 * frame_count, feeds), jnp.bfloat16),
        in_specs=[anywhere] * 3,
        out_specs=anywhere,
        scratch_shapes=[
            pltpu.VMEM((frame_count, feeds, fft_len), jnp.bfloat16),
            pltpu.VMEM((tap_count, fft_len), jnp.float32),
            pltpu.VMEM((cols, fft_len), jnp.float32),
            pltpu.VMEM((PARTS * tap_count * cols, fft_len), jnp.bfloat16),
            pltpu.VMEM((frame_count, tap_count * cols, feeds), jnp.float32),
            pltpu.VMEM((cols, frame_count, feeds), jnp.float32),
            pltpu.VMEM((channels, 2 * frame_count, feeds), jnp.bfloat16),
            pltpu.VMEM((edge, cols, feeds), jnp.float32),
            pltpu.VMEM((edge, cols, feeds), jnp.float32),
            pltpu.SemaphoreType.DMA((frame_count * CHUNKS,)),
            pltpu.SemaphoreType.DMA((2,)),
            pltpu.SemaphoreType.DMA((2,)),
            pltpu.SemaphoreType.DMA((devices,)),
            pltpu.SemaphoreType.DMA((devices,)),
            pltpu.SemaphoreType.DMA,
        ],
        compiler_params=pltpu.CompilerParams(
            collective_id=0, has_side_effects=True, vmem_limit_bytes=56 * 2**20
        ),
        name="channelize",
    )(samples, pfb_taps, table)
    block_rows = ROWS_DEV // 4
    return pl.pallas_call(
        functools.partial(correlate_kernel, devices),
        out_shape=jax.ShapeDtypeStruct((ROWS_DEV, 2 * total_feeds), jnp.float32),
        grid=(ROWS_DEV // block_rows,),
        in_specs=[pl.BlockSpec(gathered.shape, lambda i: (0, 0, 0))],
        out_specs=pl.BlockSpec((block_rows, 2 * total_feeds), lambda i: (i, 0)),
        scratch_shapes=[pltpu.VMEM((TIME_BLOCKS * 2 * frame_count, 2 * total_feeds), jnp.bfloat16)],
        compiler_params=pltpu.CompilerParams(vmem_limit_bytes=32 * 2**20),
        name="correlate",
    )(gathered)


def solution(mesh):
    placed = (P(("grp", "feed"), None, None), P())
    return jax.shard_map(
        body, mesh=mesh, in_specs=placed, out_specs=P(("grp", "feed"), None), check_vma=False
    )
```

time: 727 us -> 37.3 us (0.05)
  starting transfers between devices: 292 us -> 0 us
  waiting for transfers between devices: 272 us -> 0 us
  matrix products: 90.6 us -> 0 us
  local copies, waits for them, and re-layouts: 69.9 us -> 0.9 us
  Pallas kernels: 0 us -> 36.2 us
    all_to_all x1 -> x0, starting transfers between devices: 281 us -> none  [body(): lax.all_to_all(outgoing_all, 'feed', split_axis=0, concat_axis=0, tiled=T...]
    ppermute x1 -> x0, waiting for transfers between devices: 264 us -> none  [passed_along(): lax.ppermute(value, axis, [(source, source + steps) for source in range(f...]
    dot_general x2 -> x0, matrix products: 90.6 us -> none  [the longest x1 86 us: apply_table(): jnp.dot(filtered.reshape(feed_count * count, fft_len), dft_table, precisi...]
    pallas_call x0 -> x2, Pallas kernels: none -> 36.2 us  [the longest x1 31.9 us: body(): pl.pallas_call(functools.partial(channelize_kernel, devices), out_shape=j...]
    reshape x3 -> x0, local copies, waits for them, and re-layouts: 29.4 us -> none  [the longest x1 29.4 us: body(): frames = samples.reshape(feed_count, frame_count, fft_len)]
    unnamed x4 -> x2, local copies, waits for them, and re-layouts: 29.2 us -> 0.9 us
    slice x2 -> x0, local copies, waits for them, and re-layouts: 10.6 us -> none  [the longest x1 10.5 us: body(): tail_frames = frames[:, frame_count - edge:]]
    ppermute x1 -> x0, starting transfers between devices: 10.4 us -> none  [passed_along(): lax.ppermute(value, axis, [(source, source + steps) for source in range(f...]
  transfers between devices with their start and end apart: 2 -> 0, of which waited for: 2 -> 0; matrix products, arithmetic and copies ran while one was open for 0% -> 0% of each run, Pallas kernels for 0% -> 0%
where the time goes in v1:
time: 37.3 us; the launch traced here: 37.1 us
  Pallas kernels  36.2 us (97%)
  local copies, waits for them, and re-layouts  0.9 us (2%)
    pallas_call x1, Pallas kernels, body(): pl.pallas_call(functools.partial(channelize_kernel, devices), out_shape=j...  31.9 us
    pallas_call x1, Pallas kernels, body(): pl.pallas_call(functools.partial(correlate_kernel, devices), out_shape=ja...  4.26 us
    unnamed x2, local copies, waits for them, and re-layouts  0.9 us

profile of v1, /device:TPU:0, one launch (start us, length us, event | category | flops | bytes accessed | tf_op | source)
XLA Modules:
  0.0 37.1 jit_solution(15433290981739627570)
XLA Ops:
  0.0 31.9 %channelize.1.gathered_ref = bf16[16,16,256]{2,1,0:T(8,128)(2,1)} custom-call(bf16[1,256,65536]{2,1,0:T(8,128)(2,1)} %samples_ref.1, f32[4,8192]{1,0:T(4,128)} %taps_ref.1, f32[8,8192]{1,0:T(8,128)} %constant.2.clone.table_ref), custom_call_target="tpu_custom_call" | custom-call | tf_op jit(solution)/shard_map/channelize/pallas_call | solution.py:206
  31.9 0.0 copy-start
  31.9 0.9 %copy-done = bf16[16,16,256]{2,1,0:T(8,128)(2,1)S(1)} copy-done((bf16[16,16,256]{2,1,0:T(8,128)(2,1)S(1)}, bf16[16,16,256]{2,1,0:T(8,128)(2,1)}, u32[]{:S(2)}) %copy-start) | copy-done | bytes 131096
  32.8 4.3 %correlate.1 = f32[512,4096]{1,0:T(8,128)} custom-call(bf16[16,16,256]{2,1,0:T(8,128)(2,1)S(1)} %copy-done), custom_call_target="tpu_custom_call" | custom-call | tf_op jit(solution)/shard_map/correlate/pallas_call | solution.py:234
Async XLA Ops:
  31.9 0.9 %copy-start = (bf16[16,16,256]{2,1,0:T(8,128)(2,1)S(1)}, bf16[16,16,256]{2,1,0:T(8,128)(2,1)}, u32[]{:S(2)}) copy-start(bf16[16,16,256]{2,1,0:T(8,128)(2,1)} %channelize.1.gathered_ref) | copy-start | bytes 393220

commit v2 on v1

--- a/solution.py
+++ b/solution.py
@@ -13,7 +13,8 @@
 TIME_BLOCKS = 2
 ROWS_DEV = 512
 PARTS = 3
-CHUNKS = 4
+CHUNKS = 8
+GROUPS = 2
 
 
 def dft_rows(fft_len, channels):
@@ -24,7 +25,7 @@
 
 def channelize_kernel(
     devices, samples_ref, taps_ref, table_ref, out_ref,
-    frames_buf, taps_buf, table_buf, w_buf, g_buf, spec_buf, msg_buf, spill_out, spill_in,
+    frames_buf, taps_buf, table_buf, w_buf, g_buf, spec_buf, msg_buf, spill_out, spill_in, acc_buf,
     load_sems, aux_sems, spill_sems, send_sems, recv_sems, own_sem,
 ):
     me = lax.axis_index("feed")
@@ -45,21 +46,24 @@
     for copy in aux:
         copy.start()
 
+    group_frames = frame_count // GROUPS
+
     def load(frame, part):
         start = pl.multiple_of(frame * fft_len + part * chunk, 128)
+        here = pl.multiple_of(part * chunk, 128)
         return pltpu.make_async_copy(
             samples_ref.at[0, :, pl.ds(start, chunk)],
-            frames_buf.at[frame, :, pl.ds(part * chunk, chunk)],
+            frames_buf.at[frame, :, pl.ds(here, chunk)],
             load_sems.at[frame * CHUNKS + part],
         )
 
-    def start_frame(step, carry):
-        frame = lax.rem(step + early, frame_count)
-        for part in range(CHUNKS):
-            load(frame, part).start()
-        return carry
-
-    lax.fori_loop(0, frame_count, start_frame, 0)
+    def start_part(step, carry):
+        group = GROUPS - 1 - step // CHUNKS
+        for inner in range(group_frames):
+            load(group * group_frames + inner, lax.rem(step, CHUNKS)).start()
+        return carry
+
+    lax.fori_loop(0, GROUPS * CHUNKS, start_part, 0)
 
     barrier = pltpu.get_barrier_semaphore()
 
@@ -72,34 +76,46 @@
 
     for copy in aux:
         copy.wait()
-    for tap in range(tap_count):
-        rest = taps_buf[tap : tap + 1, :] * table_buf[...]
-        for part in range(PARTS):
-            piece = rest.astype(jnp.bfloat16)
-            row = (part * tap_count + tap) * cols
-            w_buf[row : row + cols, :] = piece
-            rest = rest - piece.astype(jnp.float32)
-
+    def build(part):
+        for block in range(chunk // 256):
+            lines = pl.ds(part * chunk + block * 256, 256)
+            pieces = [[] for _ in range(PARTS)]
+            for tap in range(tap_count):
+                rest = taps_buf[tap : tap + 1, lines] * table_buf[:, lines]
+                for index in range(PARTS):
+                    piece = rest.astype(jnp.bfloat16).astype(jnp.float32)
+                    pieces[index].append(piece)
+                    rest = rest - piece
+            w_buf[lines, :] = jnp.concatenate(sum(pieces, []), axis=0).T.astype(jnp.bfloat16)
+
+    def do_part(group, part, first):
+        begin = group * group_frames
+        for inner in range(group_frames):
+            load(begin + inner, part).wait()
+        lines = pl.ds(part * chunk if isinstance(part, int) else pl.multiple_of(part * chunk, 128), chunk)
+        block = frames_buf[begin : begin + group_frames, :, lines]
+        product = jnp.dot(
+            block.reshape(group_frames * feeds, chunk), w_buf[lines, :],
+            preferred_element_type=jnp.float32,
+        )
+        acc_buf[...] = product if first else acc_buf[...] + product
+
+    def end_group(group):
+        rows = tap_count * cols
+        for inner in range(group_frames):
+            total = acc_buf[inner * feeds : (inner + 1) * feeds, :].T
+            summed = total[:rows]
+            for index in range(1, PARTS):
+                summed = summed + total[index * rows : (index + 1) * rows]
+            g_buf[group * group_frames + inner] = summed
+
+    build(0)
+    for part in range(CHUNKS):
+        if part + 1 < CHUNKS:
+            build(part + 1)
+        do_part(GROUPS - 1, part, part == 0)
+    end_group(GROUPS - 1)
     pl.semaphore_wait(barrier, devices - 1)
-
-    def do_frame(frame, carry):
-        total = None
-        for part in range(CHUNKS):
-            load(frame, part).wait()
-            columns = slice(part * chunk, (part + 1) * chunk)
-            product = lax.dot_general(
-                w_buf[:, columns], frames_buf[frame, :, columns],
-                (((1,), (1,)), ((), ())), preferred_element_type=jnp.float32,
-            )
-            total = product if total is None else total + product
-        rows = tap_count * cols
-        summed = total[:rows]
-        for part in range(1, PARTS):
-            summed = summed + total[part * rows : (part + 1) * rows]
-        g_buf[frame] = summed
-        return carry
-
-    lax.fori_loop(early, frame_count, do_frame, 0)
 
     for later in range(edge):
         total = g_buf[early + later, 0:cols, :]
@@ -116,7 +132,15 @@
         spill.start()
         spill_in[...] = jnp.zeros_like(spill_in)
 
-    lax.fori_loop(0, early, do_frame, 0)
+    for group in reversed(range(GROUPS - 1)):
+        do_part(group, 0, True)
+
+        def more(part, carry):
+            do_part(group, part, False)
+            return carry
+
+        lax.fori_loop(1, CHUNKS, more, 0)
+        end_group(group)
 
     @pl.when(me < span)
     def _():
@@ -212,12 +236,13 @@
             pltpu.VMEM((frame_count, feeds, fft_len), jnp.bfloat16),
             pltpu.VMEM((tap_count, fft_len), jnp.float32),
             pltpu.VMEM((cols, fft_len), jnp.float32),
-            pltpu.VMEM((PARTS * tap_count * cols, fft_len), jnp.bfloat16),
+            pltpu.VMEM((fft_len, PARTS * tap_count * cols), jnp.bfloat16),
             pltpu.VMEM((frame_count, tap_count * cols, feeds), jnp.float32),
             pltpu.VMEM((cols, frame_count, feeds), jnp.float32),
             pltpu.VMEM((channels, 2 * frame_count, feeds), jnp.bfloat16),
             pltpu.VMEM((edge, cols, feeds), jnp.float32),
             pltpu.VMEM((edge, cols, feeds), jnp.float32),
+            pltpu.VMEM((frame_count // GROUPS * feeds, PARTS * tap_count * cols), jnp.float32),
             pltpu.SemaphoreType.DMA((frame_count * CHUNKS,)),
             pltpu.SemaphoreType.DMA((2,)),
             pltpu.SemaphoreType.DMA((2,)),

time: 37.3 us -> 28.7 us (0.77)
  Pallas kernels: 36.2 us -> 27.6 us
    pallas_call x1, Pallas kernels: 31.9 us -> 23.4 us  [body(): pl.pallas_call(functools.partial(channelize_kernel, devices), out_shape=j...]
where the time goes in v2:
time: 28.7 us; the launch traced here: 28.6 us
  Pallas kernels  27.6 us (96%)
  local copies, waits for them, and re-layouts  0.9 us (3%)
    pallas_call x1, Pallas kernels, body(): pl.pallas_call(functools.partial(channelize_kernel, devices), out_shape=j...  23.4 us
    pallas_call x1, Pallas kernels, body(): pl.pallas_call(functools.partial(correlate_kernel, devices), out_shape=ja...  4.27 us
    unnamed x2, local copies, waits for them, and re-layouts  0.9 us

profile of v2, /device:TPU:0, one launch (start us, length us, event | category | flops | bytes accessed | tf_op | source)
XLA Modules:
  0.0 28.6 jit_solution(6335136364389657776)
XLA Ops:
  0.0 23.4 %channelize.1.gathered_ref = bf16[16,16,256]{2,1,0:T(8,128)(2,1)} custom-call(bf16[1,256,65536]{2,1,0:T(8,128)(2,1)} %samples_ref.1, f32[4,8192]{1,0:T(4,128)} %taps_ref.1, f32[8,8192]{1,0:T(8,128)} %constant.2.clone.table_ref), custom_call_target="tpu_custom_call" | custom-call | tf_op jit(solution)/shard_map/channelize/pallas_call | solution.py:230
  23.4 0.0 copy-start
  23.4 0.9 %copy-done = bf16[16,16,256]{2,1,0:T(8,128)(2,1)S(1)} copy-done((bf16[16,16,256]{2,1,0:T(8,128)(2,1)S(1)}, bf16[16,16,256]{2,1,0:T(8,128)(2,1)}, u32[]{:S(2)}) %copy-start) | copy-done | bytes 131096
  24.3 4.3 %correlate.1 = f32[512,4096]{1,0:T(8,128)} custom-call(bf16[16,16,256]{2,1,0:T(8,128)(2,1)S(1)} %copy-done), custom_call_target="tpu_custom_call" | custom-call | tf_op jit(solution)/shard_map/correlate/pallas_call | solution.py:259
Async XLA Ops:
  23.4 0.9 %copy-start = (bf16[16,16,256]{2,1,0:T(8,128)(2,1)S(1)}, bf16[16,16,256]{2,1,0:T(8,128)(2,1)}, u32[]{:S(2)}) copy-start(bf16[16,16,256]{2,1,0:T(8,128)(2,1)} %channelize.1.gathered_ref) | copy-start | bytes 393220

commit v3 on v2

--- a/solution.py
+++ b/solution.py
@@ -202,18 +202,23 @@
     def _():
         for block in range(TIME_BLOCKS):
             for group in range(span):
-                piece = gathered_ref[block * span + group]
-                wide = piece.astype(jnp.float32)
-                turned = jnp.concatenate([-wide[half:], wide[:half]], axis=0).astype(jnp.bfloat16)
-                lines = slice(block * depth, (block + 1) * depth)
-                right_buf[lines, group * feeds : (group + 1) * feeds] = piece
-                right_buf[lines, total_feeds + group * feeds : total_feeds + (group + 1) * feeds] = turned
+                right_buf[
+                    block * depth : (block + 1) * depth, group * feeds : (group + 1) * feeds
+                ] = gathered_ref[block * span + group]
 
     start = pl.multiple_of(lax.rem(me, owners) * ROWS_DEV + pl.program_id(0) * rows, 128)
     left = right_buf[:, pl.ds(start, rows)]
-    out_ref[...] = lax.dot_general(
-        left, right_buf[...], (((0,), (0,)), ((), ())), preferred_element_type=jnp.float32
+    wide = left.astype(jnp.float32)
+    turned = []
+    for block in range(TIME_BLOCKS):
+        middle = block * depth + half
+        turned += [wide[middle : middle + half], -wide[middle - half : middle]]
+    both = jnp.concatenate([left, jnp.concatenate(turned, axis=0).astype(jnp.bfloat16)], axis=1)
+    product = lax.dot_general(
+        both, right_buf[...], (((0,), (0,)), ((), ())), preferred_element_type=jnp.float32
     ) * (1.0 / spectra_count)
+    out_ref[:, :total_feeds] = product[:rows]
+    out_ref[:, total_feeds:] = product[rows:]
 
 
 def body(samples, pfb_taps):
@@ -229,9 +234,9 @@
     anywhere = pl.BlockSpec(memory_space=pl.ANY)
     gathered = pl.pallas_call(
         functools.partial(channelize_kernel, devices),
-        out_shape=jax.ShapeDtypeStruct((devices, 2 * frame_count, feeds), jnp.bfloat16),
+        out_shape=pltpu.VMEM((devices, 2 * frame_count, feeds), jnp.bfloat16),
         in_specs=[anywhere] * 3,
-        out_specs=anywhere,
+        out_specs=pl.BlockSpec(memory_space=pltpu.VMEM),
         scratch_shapes=[
             pltpu.VMEM((frame_count, feeds, fft_len), jnp.bfloat16),
             pltpu.VMEM((tap_count, fft_len), jnp.float32),
@@ -262,7 +267,7 @@
         grid=(ROWS_DEV // block_rows,),
         in_specs=[pl.BlockSpec(gathered.shape, lambda i: (0, 0, 0))],
         out_specs=pl.BlockSpec((block_rows, 2 * total_feeds), lambda i: (i, 0)),
-        scratch_shapes=[pltpu.VMEM((TIME_BLOCKS * 2 * frame_count, 2 * total_feeds), jnp.bfloat16)],
+        scratch_shapes=[pltpu.VMEM((TIME_BLOCKS * 2 * frame_count, total_feeds), jnp.bfloat16)],
         compiler_params=pltpu.CompilerParams(vmem_limit_bytes=32 * 2**20),
         name="correlate",
     )(gathered)

time: 28.7 us -> 27.7 us (0.965)
  local copies, waits for them, and re-layouts: 0.9 us -> 0 us
    unnamed x2 -> x0, local copies, waits for them, and re-layouts: 0.9 us -> none
where the time goes in v3:
time: 27.7 us; the launch traced here: 27.6 us
  Pallas kernels  27.5 us (99%)
    pallas_call x1, Pallas kernels, body(): pl.pallas_call(functools.partial(channelize_kernel, devices), out_shape=p...  23.3 us
    pallas_call x1, Pallas kernels, body(): pl.pallas_call(functools.partial(correlate_kernel, devices), out_shape=ja...  4.28 us

profile of v3, /device:TPU:0, one launch (start us, length us, event | category | flops | bytes accessed | tf_op | source)
XLA Modules:
  0.0 27.6 jit_solution(6524653427225047774)
XLA Ops:
  0.0 23.3 %channelize.1.gathered_ref = bf16[16,16,256]{2,1,0:T(8,128)(2,1)S(1)} custom-call(bf16[1,256,65536]{2,1,0:T(8,128)(2,1)} %samples_ref.1, f32[4,8192]{1,0:T(4,128)} %taps_ref.1, f32[8,8192]{1,0:T(8,128)} %constant.2.clone.table_ref), custom_call_target="tpu_custom_call" | custom-call | tf_op jit(solution)/shard_map/channelize/pallas_call | solution.py:235
  23.3 4.3 %correlate.1 = f32[512,4096]{1,0:T(8,128)} custom-call(bf16[16,16,256]{2,1,0:T(8,128)(2,1)S(1)} %channelize.1.gathered_ref), custom_call_target="tpu_custom_call" | custom-call | tf_op jit(solution)/shard_map/correlate/pallas_call | solution.py:264
